TPU v7x, 32 devices: a whole 2x2x4 slice. The times are simulated.
32 devices in a mesh: freq: 4 (over z), tm: 2 (over core), beam: 4 (over y, x).
Axes of the slice: x: 2, y: 2, z: 4, core: 2. Of those that a mesh axis runs over, the one named last changes fastest.
Arguments:
- intensity: bfloat16 [4, 4096, 512], P('beam', 'freq', 'tm'), parts along dimension 0, may hold values from -32 to 32
- delay_tables: int32 [3, 12, 2048], replicated, may hold values from 0 to 511, as said below
- box_widths: int32 [8], replicated, may hold values from 1 to 128
Outputs:
- snr: float32 [4, 1024, 8, 512], P('beam', 'freq', None, 'tm'), parts along dimension 0
There are 4 independent parts, one for each index of `beam`. A program takes and returns all parts, laid end to end along the dimension named above; an argument that names none is the same for every part. Nothing has to cross between parts.
Inputs may be any that keep to these rules, and one draw needn't show every extreme that they name: `delay_tables`: at merge level s (second index s - 1), with D_s = max(1, 2^(s-2)), entry [k, s-1, b D_s + d] belongs to band b and trial d; the trials (k = 0, 1) and the delay (k = 2) lie in 0 to D_(s-1) - 1; columns from (4096 / 2^s) D_s on are not read.
All inputs are finite; a program needn't handle non-finite values.
Results may differ from a plain program's by a relative error of at most 0.0003.
Values may be sent and summed in bfloat16 or wider, within the bound.
A program may use at most 64 MiB of HBM per device.

v0:
```python
import jax
import jax.numpy as jnp
from jax import lax
from jax.sharding import PartitionSpec as P

LEVELS = 12
WMAX = 128
EPSILON = 1e-05
BANDS = ("freq", "tm")


def band_count():
    return lax.axis_size("freq") * lax.axis_size("tm")


def swapped(block, stride):
    count = band_count()
    route = []
    for low in range(count):
        high = low | 1 << stride
        if high != low and high < count:
            route += [(low, high), (high, low)]
    return lax.ppermute(block, BANDS, route)


def trial_depth(merge_level):
    if merge_level >= 2:
        return 2 ** (merge_level - 2)
    return 1


def shift_rows(source, delays, columns, largest):
    result = source
    for bit_index in range(max(largest, 0).bit_length()):
        step_size = 1 << bit_index
        moved = jnp.concatenate(
            [result[..., step_size:], jnp.zeros_like(result[..., :step_size])], axis=-1
        )
        flag = delays >> bit_index & 1 == 1
        result = jnp.where(flag[None, :, None], moved, result)
    return result[..., :columns]


def merge_bands(current, delay_tables, merge_level, first_band):
    beam_count, bands_in, depth_in, columns = current.shape
    depth_out = trial_depth(merge_level)
    bands_out = bands_in // 2
    entries = lax.dynamic_slice_in_dim(
        delay_tables[:, merge_level - 1, :], first_band * depth_out, bands_out * depth_out, 1
    )
    band_base = jnp.arange(bands_out * depth_out, dtype=jnp.int32) // depth_out * depth_in
    lower_flat = current[:, 0::2].reshape(beam_count, bands_out * depth_in, columns)
    upper_flat = current[:, 1::2].reshape(beam_count, bands_out * depth_in, columns)
    picked = jnp.take(lower_flat, band_base + entries[0], axis=1)
    chosen = jnp.take(upper_flat, band_base + entries[1], axis=1)
    delayed = shift_rows(chosen, entries[2], columns, depth_in - 1)
    return (picked + delayed).reshape(beam_count, bands_out, depth_out, columns)


def merge_across(current, delay_tables, merge_level, cross_step, device_pos):
    beam_count, rows_held, columns = current.shape
    depth_in = rows_held * 2**cross_step
    depth_out = trial_depth(merge_level)
    group_size = 2 ** (cross_step + 1)
    position = device_pos % group_size
    upper_side = position // (group_size // 2)
    row_offset = position % (group_size // 2) * rows_held
    band_index = device_pos // group_size
    entries = lax.dynamic_slice_in_dim(
        delay_tables[:, merge_level - 1, :], band_index * depth_out, depth_out, 1
    )
    lower_local = entries[0] - row_offset
    lower_hit = (lower_local >= 0) & (lower_local < rows_held) & (upper_side == 0)
    lower_rows = jnp.take(current, jnp.clip(lower_local, 0, rows_held - 1), axis=1)
    upper_local = entries[1] - row_offset
    upper_hit = (upper_local >= 0) & (upper_local < rows_held) & (upper_side == 1)
    upper_chosen = jnp.take(current, jnp.clip(upper_local, 0, rows_held - 1), axis=1)
    upper_rows = shift_rows(upper_chosen, entries[2], columns, depth_in - 1)
    partial_value = jnp.where(lower_hit[None, :, None], lower_rows, 0.0) + jnp.where(
        upper_hit[None, :, None], upper_rows, 0.0
    )
    for bit_index in range(cross_step + 1):
        blocks = partial_value.shape[1] // rows_held
        paired = partial_value.reshape(beam_count, blocks // 2, 2, rows_held, columns)
        chosen_bit = device_pos >> bit_index & 1
        kept_rows = lax.dynamic_index_in_dim(paired, chosen_bit, 2, keepdims=False)
        given_rows = lax.dynamic_index_in_dim(paired, 1 - chosen_bit, 2, keepdims=False)
        partial_value = (kept_rows + swapped(given_rows, bit_index)).reshape(
            beam_count, blocks // 2 * rows_held, columns
        )
    return partial_value


def own_trials(current, delay_tables, device_pos):
    beam_count, bands_in, depth_in, columns = current.shape
    rows = trial_depth(LEVELS) // band_count()
    entries = lax.dynamic_slice_in_dim(delay_tables[:, LEVELS - 1, :], device_pos * rows, rows, 1)
    picked = jnp.take(current[:, 0], entries[0], axis=1)
    chosen = jnp.take(current[:, 1], entries[1], axis=1)
    delayed = shift_rows(chosen, entries[2], columns, depth_in - 1)
    return picked + delayed


def body(intensity, delay_tables, box_widths):
    time_parts = lax.axis_size("tm")
    time_pos = lax.axis_index("tm")
    device_pos = lax.axis_index("freq") * time_parts + time_pos
    block_len = intensity.shape[2]
    whole_rows = lax.all_to_all(intensity, "tm", 1, 2, tiled=True)
    beam_count, channels_held, time_total = whole_rows.shape
    local_levels = channels_held.bit_length() - 1
    current = whole_rows.astype(jnp.float32)[:, :, None, :]
    for merge_level in range(1, local_levels + 1):
        current = merge_bands(
            current, delay_tables, merge_level, device_pos * (channels_held >> merge_level)
        )
    merged_levels = local_levels
    if merged_levels < LEVELS:
        current = lax.all_gather(current, BANDS, axis=1, tiled=True)
        for merge_level in range(merged_levels + 1, LEVELS):
            current = merge_bands(current, delay_tables, merge_level, 0)
        dedispersed = own_trials(current, delay_tables, device_pos)
    else:
        dedispersed = current[:, 0]
    average = jnp.sum(dedispersed, axis=-1) / time_total
    deviation = dedispersed - average[..., None]
    spread = jnp.sum(deviation * deviation, axis=-1) / time_total
    inverse = lax.rsqrt(spread + EPSILON)
    scaled = deviation * inverse[..., None]
    scaled = lax.all_gather(scaled, "tm", axis=1, tiled=True)
    padded = jnp.pad(scaled, ((0, 0), (0, 0), (0, WMAX)))
    window = lax.dynamic_slice_in_dim(padded, time_pos * block_len, block_len + WMAX, 2)
    running = jnp.cumsum(jnp.pad(window, ((0, 0), (0, 0), (1, 0))), axis=-1)
    leading_sum = running[..., :block_len]
    filtered = []
    for width_index in range(box_widths.shape[0]):
        ending = lax.dynamic_slice_in_dim(running, box_widths[width_index], block_len, 2)
        filtered.append(ending - leading_sum)
    boxed = jnp.stack(filtered, axis=2)
    return boxed * lax.rsqrt(box_widths.astype(jnp.float32))[None, None, :, None]


def solution(mesh):
    in_specs = (P("beam", "freq", "tm"), P(), P())
    out_specs = P("beam", "freq", None, "tm")
    return jax.shard_map(body, mesh=mesh, in_specs=in_specs, out_specs=out_specs, check_vma=False)
```

profile of v0, /device:TPU:0, one launch (start us, length us, event | category | flops | bytes accessed | tf_op | source)
XLA Modules:
  0.0 143.2 jit_solution(5230237503584928580)
XLA Ops:
  6.5 1.9 %copy.33 = bf16[1,1024,256]{2,0,1:T(2,128)(2,1)S(1)} copy(bf16[1,1024,256]{2,1,0:T(8,128)(2,1)} %param.13) | data formatting | bytes 1048576 | tf_op args[0]
  8.9 3.8 %reduce.32 = bf16[1024,256]{1,0:T(8,128)(2,1)S(1)} reduce(bf16[1024,1,256]{2,1,0:T(2,128)(2,1)S(1)} %bitcast.431, bf16[]{:T(256)} %broadcast.1330), dimensions={1}, to_apply=%bitcast.414.reduce_sub_computation | reduce | bytes 1048578
  13.6 3.5 %all-to-all-start = ((bf16[2,2,65536]{2,1,0:T(2,128)(2,1)}), bf16[2,2,65536]{2,1,0:T(2,128)(2,1)S(1)}, u32[]{:S(2)}, u32[]{:S(2)}) async-start(bf16[2,2,65536]{2,1,0:T(2,128)(2,1)} %reshape.1617), calls=%async_computation | async-start | bytes 1048576 | tf_op jit(solution)/shard_map/all_to_all | solution.py:109
  17.2 1.7 %all-to-all-done = bf16[2,2,65536]{2,1,0:T(2,128)(2,1)S(1)} async-done(((bf16[2,2,65536]{2,1,0:T(2,128)(2,1)}), bf16[2,2,65536]{2,1,0:T(2,128)(2,1)S(1)}, u32[]{:S(2)}, u32[]{:S(2)}) %all-to-all-start) | async-done | bytes 524320 | tf_op jit(solution)/shard_map/all_to_all | solution.py:109
  22.4 1.0 gather_fusion
  23.4 1.0 gather_fusion.1
  61.3 16.3 %all-gather.3.cloned.1.call-done = f32[8,128,512]{2,1,0:T(8,128)} async-done(((f32[1,128,512]{2,1,0:T(8,128)}), f32[8,128,512]{2,1,0:T(8,128)}) %all-gather.3.cloned.1.call-update) | async-done | bytes 2097168 | tf_op jit(solution)/shard_map/all_gather | solution.py:119
  77.6 1.8 %fusion.71 = (f32[1,4,128,512]{3,2,1,0:T(8,128)S(1)}, f32[1,4,128,512]{3,2,1,0:T(8,128)S(1)}) fusion(f32[1,8,128,512]{3,2,1,0:T(8,128)} %bitcast.434), kind=kLoop, calls=%fused_computation.354 | loop fusion | bytes 4194304 | tf_op jit(solution)/shard_map/slice | solution.py:53
  79.4 4.9 %gather_fusion.19 = f32[1024,512]{1,0:T(8,128)} fusion(f32[512,512]{1,0:T(8,128)S(1)} %bitcast.417, s32[1024]{0:T(1024)S(1)} %broadcast_clamp_fusion.2), kind=kCustom, calls=%fused_computation.20.clone | custom fusion | bytes 4198400 | tf_op jit(solution)/shard_map/jit(_take)/gather | solution.py:55
  84.3 1.8 %bitcast_select_fusion.2 = f32[1,1024,512]{2,1,0:T(8,128)S(1)} fusion(f32[1024,512]{1,0:T(8,128)} %gather_fusion.19, pred[1024]{0:T(1024)(128)(4,1)S(1)} %compare_and_fusion.2), kind=kLoop, calls=%fused_computation.27 | loop fusion | flops 524288 | bytes 4195328 | tf_op jit(solution)/shard_map/jit(_take)/select_n | solution.py:55
  86.7 1.0 copy-done
  87.7 1.2 pad_select_fusion.12
  93.3 2.0 %slice.621 = f32[1,1024,448]{2,1,0:T(8,128)} slice(f32[1,1024,512]{2,1,0:T(8,128)S(1)} %pad_select_fusion.7), slice={[0:1], [0:1024], [64:512]} | slice | bytes 3670016 | tf_op jit(solution)/shard_map/slice | solution.py:37
  95.3 4.9 %gather_fusion.18 = f32[1024,512]{1,0:T(8,128)} fusion(f32[512,512]{1,0:T(8,128)S(1)} %bitcast.416, s32[1024]{0:T(1024)S(1)} %broadcast_clamp_fusion.3), kind=kCustom, calls=%fused_computation.3.clone | custom fusion | bytes 4198400 | tf_op jit(solution)/shard_map/jit(_take)/gather | solution.py:54
  100.2 2.6 %fusion.1 = f32[1,1024,512]{2,1,0:T(8,128)S(1)} fusion(f32[1024,512]{1,0:T(8,128)} %gather_fusion.18, f32[1,1024,512]{2,1,0:T(8,128)S(1)} %pad_select_fusion.7, f32[1,1024,448]{2,1,0:T(8,128)} %slice.621, pred[1024]{0:T(1024)(128)(4,1)S(1)} %compare_and_fusion.3, pred[1024]{0:T(1024)(128)(4,1)S(1)} %get-tuple-element.18), kind=kLoop, calls=%fused_computation.29 | loop fusion | flops 1572864 | bytes 8128512 | tf_op jit(solution)/shard_map/add | solution.py:57
  102.9 4.9 %gather_fusion.21 = f32[1024,512]{1,0:T(8,128)} fusion(f32[512,512]{1,0:T(8,128)S(1)} %bitcast.418, s32[1024]{0:T(1024)S(1)} %broadcast_clamp_fusion), kind=kCustom, calls=%fused_computation.22.clone | custom fusion | bytes 4198400 | tf_op jit(solution)/shard_map/jit(_take)/gather | solution.py:55
  107.8 1.8 %bitcast_select_fusion = f32[1,1024,512]{2,1,0:T(8,128)S(1)} fusion(f32[1024,512]{1,0:T(8,128)} %gather_fusion.21, pred[1024]{0:T(1024)(128)(4,1)S(1)} %compare_and_fusion), kind=kLoop, calls=%fused_computation.24 | loop fusion | flops 524288 | bytes 4195328 | tf_op jit(solution)/shard_map/jit(_take)/select_n | solution.py:55
  110.2 1.0 copy-done.1
  111.2 1.3 pad_select_fusion.6
  117.8 1.3 slice.631
  119.1 4.9 %gather_fusion.20 = f32[1024,512]{1,0:T(8,128)} fusion(f32[512,512]{1,0:T(8,128)S(1)} %bitcast.415, s32[1024]{0:T(1024)S(1)} %broadcast_clamp_fusion.1), kind=kCustom, calls=%fused_computation.21.clone | custom fusion | bytes 4198400 | tf_op jit(solution)/shard_map/jit(_take)/gather | solution.py:54
  123.9 2.4 %fusion = f32[1,1024,512]{2,1,0:T(8,128)S(1)} fusion(f32[1024,512]{1,0:T(8,128)} %gather_fusion.20, f32[1,1024,512]{2,1,0:T(8,128)S(1)} %pad_select_fusion, f32[1,1024,384]{2,1,0:T(8,128)} %slice.631, pred[1024]{0:T(1024)(128)(4,1)S(1)} %compare_and_fusion.1, pred[1024]{0:T(1024)(128)(4,1)S(1)} %get-tuple-element.6), kind=kLoop, calls=%fused_computation.26 | loop fusion | flops 1572864 | bytes 7866368 | tf_op jit(solution)/shard_map/add | solution.py:57
  130.4 2.2 %all_gather.7 = f32[1,256,512]{2,1,0:T(8,128)S(1)} all-gather(f32[1,128,512]{2,1,0:T(8,128)S(1)} %subtract_multiply_fusion), channel_id=1, replica_groups=mesh['freq'=4,'tm'=2,'beam'=4] {'tm'}, dimensions={1}, use_global_device_ids=true | all-gather | bytes 786432 | tf_op jit(solution)/shard_map/all_gather | solution.py:130
  134.4 2.0 %copy.25 = f32[1,256,8,256]{3,2,1,0:T(8,128)} copy(f32[1,256,8,256]{1,3,2,0:T(8,128)S(1)} %broadcast_multiply_fusion) | data formatting | bytes 4194304 | tf_op jit(solution)/shard_map/mul | solution.py:140
  (221 shorter events, 43.0 us)
Async XLA Ops:
  13.6 5.2 %all-to-all-start = ((bf16[2,2,65536]{2,1,0:T(2,128)(2,1)}), bf16[2,2,65536]{2,1,0:T(2,128)(2,1)S(1)}, u32[]{:S(2)}, u32[]{:S(2)}) async-start(bf16[2,2,65536]{2,1,0:T(2,128)(2,1)} %reshape.1617), calls=%async_computation | async-start | bytes 1048576 | tf_op jit(solution)/shard_map/all_to_all | solution.py:109
  17.1 60.5 %all-gather.3.cloned.1.call-start = ((), (), s32[]{:S(2)}) async-start(), calls=%async_computation.1 | async-start | bytes 2359296 | tf_op jit(solution)/shard_map/all_gather | solution.py:119
  20.1 2.0 %copy-start.2 = (s32[3,12,2048]{2,1,0:T(8,128)S(1)}, s32[3,12,2048]{2,1,0:T(8,128)}, u32[]{:S(2)}) copy-start(s32[3,12,2048]{2,1,0:T(8,128)} %param.14) | copy-start | bytes 884740
  43.8 1.8 %copy-start.3 = (s32[8]{0:T(128)S(1)}, s32[8]{0:T(128)}, u32[]{:S(2)}) copy-start(s32[8]{0:T(128)} %param.15) | copy-start | bytes 100
  86.1 1.6 %copy-start = (f32[1024,512]{1,0:T(8,128)S(1)}, f32[1024,512]{1,0:T(8,128)}, u32[]{:S(2)}) copy-start(f32[1024,512]{1,0:T(8,128)} %gather_fusion.19) | copy-start | bytes 6291460
  109.6 1.6 %copy-start.1 = (f32[1024,512]{1,0:T(8,128)S(1)}, f32[1024,512]{1,0:T(8,128)}, u32[]{:S(2)}) copy-start(f32[1024,512]{1,0:T(8,128)} %gather_fusion.21) | copy-start | bytes 6291460
Sparse Core Ops, SparseCore 0:
  45.7 31.8 all-gather.2
where the time goes:
time: 144 us; the launch traced here: 143 us
  local copies, waits for them, and re-layouts  65.7 us (46%)
  between operations  29.5 us (20%)
  other arithmetic  24.3 us (17%)
  waiting for transfers between devices  18 us (12%)
  starting transfers between devices  3.53 us (2%)
  blocking collectives  2.18 us (2%)
    gather x11, local copies, waits for them, and re-layouts, merge_bands(): chosen = jnp.take(upper_flat, band_base + entries[1], axis=1)  16.8 us
    gather x11, local copies, waits for them, and re-layouts, merge_bands(): picked = jnp.take(lower_flat, band_base + entries[0], axis=1)  16.8 us
    all_gather x1, waiting for transfers between devices, body(): current = lax.all_gather(current, BANDS, axis=1, tiled=True)  16.3 us
    slice x45, local copies, waits for them, and re-layouts, shift_rows(): result[..., step_size:]  14.7 us
    select_n x36, other arithmetic, shift_rows(): result = jnp.where(flag[None, :, None], moved, result)  7.66 us
    add x8, other arithmetic, merge_bands(): return (picked + delayed).reshape(beam_count, bands_out, depth_out, columns)  6.29 us
    unnamed x12, local copies, waits for them, and re-layouts  5.69 us
    unnamed x8, other arithmetic  4.18 us
  transfers between devices with their start and end apart: 2, of which 2 were waited for; matrix products, arithmetic and copies ran while one was open for 1% of the time, Pallas kernels for 0%

commit v1 on v0

--- a/solution.py
+++ b/solution.py
@@ -7,6 +7,14 @@
 WMAX = 128
 EPSILON = 1e-05
 BANDS = ("freq", "tm")
+
+
+def roads_wait(shard_in):
+    u1 = lax.psum(1, axis_name="tm")
+    latest = jnp.split(shard_in, u1, axis=1)
+    out_arr = jnp.stack(latest, axis=0)
+    spare = lax.all_to_all(out_arr, concat_axis=0, split_axis=0, axis_name="tm")
+    return jnp.concatenate(spare, axis=2)
 
 
 def band_count():
@@ -106,7 +114,7 @@
     time_pos = lax.axis_index("tm")
     device_pos = lax.axis_index("freq") * time_parts + time_pos
     block_len = intensity.shape[2]
-    whole_rows = lax.all_to_all(intensity, "tm", 1, 2, tiled=True)
+    whole_rows = roads_wait(intensity)
     beam_count, channels_held, time_total = whole_rows.shape
     local_levels = channels_held.bit_length() - 1
     current = whole_rows.astype(jnp.float32)[:, :, None, :]

time: 144 us -> 138 us (0.958)
  other arithmetic: 24.3 us -> 21.3 us
  local copies, waits for them, and re-layouts: 65.7 us -> 62.9 us
    unnamed x8 -> x7, other arithmetic: 4.18 us -> 0.36 us
    unnamed x12 -> x8, local copies, waits for them, and re-layouts: 5.69 us -> 1.97 us
where the time goes in v1:
time: 138 us; the launch traced here: 137 us
  local copies, waits for them, and re-layouts  62.9 us (46%)
  between operations  29.5 us (21%)
  other arithmetic  21.3 us (15%)
  waiting for transfers between devices  18 us (13%)
  starting transfers between devices  3.53 us (3%)
  blocking collectives  2.18 us (2%)
    gather x11, local copies, waits for them, and re-layouts, merge_bands(): chosen = jnp.take(upper_flat, band_base + entries[1], axis=1)  16.8 us
    gather x11, local copies, waits for them, and re-layouts, merge_bands(): picked = jnp.take(lower_flat, band_base + entries[0], axis=1)  16.8 us
    all_gather x1, waiting for transfers between devices, body(): current = lax.all_gather(current, BANDS, axis=1, tiled=True)  16.3 us
    slice x45, local copies, waits for them, and re-layouts, shift_rows(): result[..., step_size:]  14.7 us
    select_n x36, other arithmetic, shift_rows(): result = jnp.where(flag[None, :, None], moved, result)  7.57 us
    add x8, other arithmetic, merge_bands(): return (picked + delayed).reshape(beam_count, bands_out, depth_out, columns)  6.29 us
    select_n x9, other arithmetic, merge_bands(): chosen = jnp.take(upper_flat, band_base + entries[1], axis=1)  4.13 us
    all_to_all x1, starting transfers between devices, roads_wait(): spare = lax.all_to_all(out_arr, concat_axis=0, split_axis=0, axis_name='tm')  3.49 us
  transfers between devices with their start and end apart: 2, of which 2 were waited for; matrix products, arithmetic and copies ran while one was open for 1% of the time, Pallas kernels for 0%

profile of v1, /device:TPU:0, one launch (start us, length us, event | category | flops | bytes accessed | tf_op | source)
XLA Modules:
  0.0 137.3 jit_solution(16406924316088087563)
XLA Ops:
  6.5 1.1 slice_bitcast_fusion.3
  7.6 0.8 pad_maximum_fusion
  8.4 3.5 %all-to-all-start = ((bf16[2,1,512,256]{3,2,1,0:T(8,128)(2,1)}), bf16[2,1,512,256]{3,2,1,0:T(8,128)(2,1)S(1)}, u32[]{:S(2)}, u32[]{:S(2)}) async-start(bf16[2,1,512,256]{3,2,1,0:T(8,128)(2,1)} %pad_maximum_fusion), calls=%async_computation | async-start | bytes 1048576 | tf_op jit(solution)/shard_map/all_to_all | solution.py:16
  12.0 1.7 %all-to-all-done = bf16[2,1,512,256]{3,2,1,0:T(8,128)(2,1)S(1)} async-done(((bf16[2,1,512,256]{3,2,1,0:T(8,128)(2,1)}), bf16[2,1,512,256]{3,2,1,0:T(8,128)(2,1)S(1)}, u32[]{:S(2)}, u32[]{:S(2)}) %all-to-all-start) | async-done | bytes 524320 | tf_op jit(solution)/shard_map/all_to_all | solution.py:16
  16.8 1.0 gather_fusion
  17.8 1.0 gather_fusion.1
  55.6 16.3 %all-gather.3.cloned.1.call-done = f32[8,128,512]{2,1,0:T(8,128)} async-done(((f32[1,128,512]{2,1,0:T(8,128)}), f32[8,128,512]{2,1,0:T(8,128)}) %all-gather.3.cloned.1.call-update) | async-done | bytes 2097168 | tf_op jit(solution)/shard_map/all_gather | solution.py:127
  71.8 1.8 %fusion.71 = (f32[1,4,128,512]{3,2,1,0:T(8,128)S(1)}, f32[1,4,128,512]{3,2,1,0:T(8,128)S(1)}) fusion(f32[1,8,128,512]{3,2,1,0:T(8,128)} %bitcast.428), kind=kLoop, calls=%fused_computation.357 | loop fusion | bytes 4194304 | tf_op jit(solution)/shard_map/slice | solution.py:61
  73.7 4.9 %gather_fusion.19 = f32[1024,512]{1,0:T(8,128)} fusion(f32[512,512]{1,0:T(8,128)S(1)} %bitcast.414, s32[1024]{0:T(1024)S(1)} %broadcast_clamp_fusion.2), kind=kCustom, calls=%fused_computation.20.clone | custom fusion | bytes 4198400 | tf_op jit(solution)/shard_map/jit(_take)/gather | solution.py:63
  78.5 1.8 %bitcast_select_fusion.2 = f32[1,1024,512]{2,1,0:T(8,128)S(1)} fusion(f32[1024,512]{1,0:T(8,128)} %gather_fusion.19, pred[1024]{0:T(1024)(128)(4,1)S(1)} %compare_and_fusion.2), kind=kLoop, calls=%fused_computation.27 | loop fusion | flops 524288 | bytes 4195328 | tf_op jit(solution)/shard_map/jit(_take)/select_n | solution.py:63
  81.0 1.0 copy-done
  81.9 1.2 pad_select_fusion.12
  87.5 2.0 %slice.621 = f32[1,1024,448]{2,1,0:T(8,128)} slice(f32[1,1024,512]{2,1,0:T(8,128)S(1)} %pad_select_fusion.7), slice={[0:1], [0:1024], [64:512]} | slice | bytes 3670016 | tf_op jit(solution)/shard_map/slice | solution.py:45
  89.5 4.9 %gather_fusion.18 = f32[1024,512]{1,0:T(8,128)} fusion(f32[512,512]{1,0:T(8,128)S(1)} %bitcast.413, s32[1024]{0:T(1024)S(1)} %broadcast_clamp_fusion.3), kind=kCustom, calls=%fused_computation.3.clone | custom fusion | bytes 4198400 | tf_op jit(solution)/shard_map/jit(_take)/gather | solution.py:62
  94.4 2.6 %fusion.1 = f32[1,1024,512]{2,1,0:T(8,128)S(1)} fusion(f32[1024,512]{1,0:T(8,128)} %gather_fusion.18, f32[1,1024,512]{2,1,0:T(8,128)S(1)} %pad_select_fusion.7, f32[1,1024,448]{2,1,0:T(8,128)} %slice.621, pred[1024]{0:T(1024)(128)(4,1)S(1)} %compare_and_fusion.3, pred[1024]{0:T(1024)(128)(4,1)S(1)} %get-tuple-element.18), kind=kLoop, calls=%fused_computation.29 | loop fusion | flops 1572864 | bytes 8128512 | tf_op jit(solution)/shard_map/add | solution.py:65
  97.1 4.9 %gather_fusion.21 = f32[1024,512]{1,0:T(8,128)} fusion(f32[512,512]{1,0:T(8,128)S(1)} %bitcast.415, s32[1024]{0:T(1024)S(1)} %broadcast_clamp_fusion), kind=kCustom, calls=%fused_computation.22.clone | custom fusion | bytes 4198400 | tf_op jit(solution)/shard_map/jit(_take)/gather | solution.py:63
  102.0 1.8 %bitcast_select_fusion = f32[1,1024,512]{2,1,0:T(8,128)S(1)} fusion(f32[1024,512]{1,0:T(8,128)} %gather_fusion.21, pred[1024]{0:T(1024)(128)(4,1)S(1)} %compare_and_fusion), kind=kLoop, calls=%fused_computation.24 | loop fusion | flops 524288 | bytes 4195328 | tf_op jit(solution)/shard_map/jit(_take)/select_n | solution.py:63
  104.4 1.0 copy-done.1
  105.4 1.2 pad_select_fusion.6
  111.9 1.3 slice.631
  113.2 4.9 %gather_fusion.20 = f32[1024,512]{1,0:T(8,128)} fusion(f32[512,512]{1,0:T(8,128)S(1)} %bitcast.412, s32[1024]{0:T(1024)S(1)} %broadcast_clamp_fusion.1), kind=kCustom, calls=%fused_computation.21.clone | custom fusion | bytes 4198400 | tf_op jit(solution)/shard_map/jit(_take)/gather | solution.py:62
  118.1 2.4 %fusion = f32[1,1024,512]{2,1,0:T(8,128)S(1)} fusion(f32[1024,512]{1,0:T(8,128)} %gather_fusion.20, f32[1,1024,512]{2,1,0:T(8,128)S(1)} %pad_select_fusion, f32[1,1024,384]{2,1,0:T(8,128)} %slice.631, pred[1024]{0:T(1024)(128)(4,1)S(1)} %compare_and_fusion.1, pred[1024]{0:T(1024)(128)(4,1)S(1)} %get-tuple-element.6), kind=kLoop, calls=%fused_computation.26 | loop fusion | flops 1572864 | bytes 7866368 | tf_op jit(solution)/shard_map/add | solution.py:65
  124.6 2.2 %all_gather.7 = f32[1,256,512]{2,1,0:T(8,128)S(1)} all-gather(f32[1,128,512]{2,1,0:T(8,128)S(1)} %subtract_multiply_fusion), channel_id=1, replica_groups=mesh['freq'=4,'tm'=2,'beam'=4] {'tm'}, dimensions={1}, use_global_device_ids=true | all-gather | bytes 786432 | tf_op jit(solution)/shard_map/all_gather | solution.py:138
  128.5 2.0 %copy.24 = f32[1,256,8,256]{3,2,1,0:T(8,128)} copy(f32[1,256,8,256]{1,3,2,0:T(8,128)S(1)} %broadcast_multiply_fusion) | data formatting | bytes 4194304 | tf_op jit(solution)/shard_map/mul | solution.py:148
  (219 shorter events, 41.0 us)
Async XLA Ops:
  8.4 5.2 %all-to-all-start = ((bf16[2,1,512,256]{3,2,1,0:T(8,128)(2,1)}), bf16[2,1,512,256]{3,2,1,0:T(8,128)(2,1)S(1)}, u32[]{:S(2)}, u32[]{:S(2)}) async-start(bf16[2,1,512,256]{3,2,1,0:T(8,128)(2,1)} %pad_maximum_fusion), calls=%async_computation | async-start | bytes 1048576 | tf_op jit(solution)/shard_map/all_to_all | solution.py:16
  11.9 59.9 %all-gather.3.cloned.1.call-start = ((), (), s32[]{:S(2)}) async-start(), calls=%async_computation.1 | async-start | bytes 2359296 | tf_op jit(solution)/shard_map/all_gather | solution.py:127
  14.6 2.0 %copy-start.2 = (s32[3,12,2048]{2,1,0:T(8,128)S(1)}, s32[3,12,2048]{2,1,0:T(8,128)}, u32[]{:S(2)}) copy-start(s32[3,12,2048]{2,1,0:T(8,128)} %param.14) | copy-start | bytes 884740
  38.0 1.8 %copy-start.3 = (s32[8]{0:T(128)S(1)}, s32[8]{0:T(128)}, u32[]{:S(2)}) copy-start(s32[8]{0:T(128)} %param.15) | copy-start | bytes 100
  80.3 1.6 %copy-start = (f32[1024,512]{1,0:T(8,128)S(1)}, f32[1024,512]{1,0:T(8,128)}, u32[]{:S(2)}) copy-start(f32[1024,512]{1,0:T(8,128)} %gather_fusion.19) | copy-start | bytes 6291460
  103.8 1.6 %copy-start.1 = (f32[1024,512]{1,0:T(8,128)S(1)}, f32[1024,512]{1,0:T(8,128)}, u32[]{:S(2)}) copy-start(f32[1024,512]{1,0:T(8,128)} %gather_fusion.21) | copy-start | bytes 6291460
Sparse Core Ops, SparseCore 0:
  39.9 31.8 all-gather.2
